TPU v7x, 32 devices: a whole 2x2x4 slice. The times are simulated.
32 devices in a mesh: band: 2 (over x), tm: 16 (over z, y, core).
Axes of the slice: x: 2, y: 2, z: 4, core: 2. Of those that a mesh axis runs over, the one named last changes fastest.
Arguments:
- voltages: bfloat16 [65536, 2048], P(('band', 'tm')), parts along dimension 0, may hold values from -6 to 6
- panel_map: int32 [2048], replicated, may hold values from 0 to 2047, each once
- block_list: int32 [16, 2], replicated, may hold values from 0 to 15, as said below
Outputs:
- visibilities: float32 [32, 2, 256, 128, 128], P('band', None, 'tm'), parts along dimension 0
There are 2 independent parts, one for each index of `band`. A program takes and returns all parts, laid end to end along the dimension named above; an argument that names none is the same for every part. Nothing has to cross between parts.
Inputs may be any that keep to these rules, and one draw needn't show every extreme that they name: `block_list`: each row is a pair of panel numbers; the list names exactly 8 distinct panels, among them panel 0 and panel 16 - 1, every one of them in its first column.
All inputs are finite; a program needn't handle non-finite values.
Results may differ from a plain program's by a relative error of at most 0.0064.
Values may be sent and summed in bfloat16 or wider, within the bound.
No kernel may reach another device: no remote copies, remote signals or barrier semaphores. Data moves between devices by JAX's collectives and lax.ppermute only.
A program may use at most 128 MiB of HBM per device.

v0:
```python
import jax
import jax.numpy as jnp
from jax import lax
from jax.sharding import PartitionSpec as P

CHANNELS = 256
TAPS = 4
PANEL = 128


def from_behind(block, axis, distance):
    devices = range(lax.axis_size(axis))
    route = [(i - distance, i) for i in devices if i - distance in devices]
    return lax.ppermute(block, axis, route)


def filter_taps(taps, frame):
    length = taps * frame
    place = jnp.arange(length).astype(jnp.float32)
    middle = (length - 1) / 2.0
    window = 0.5 - 0.5 * jnp.cos(2.0 * jnp.pi * (place + 0.5) / length)
    shape_h = jnp.sinc((place - middle) / frame) * window
    shape_h = shape_h / jnp.sqrt(jnp.sum(shape_h * shape_h))
    return shape_h.reshape(taps, frame).astype(jnp.float32)


def dft_table(channels):
    frame = 2 * channels
    rows_k = jnp.arange(channels, dtype=jnp.int32)[:, None]
    cols_n = jnp.arange(frame, dtype=jnp.int32)[None, :]
    phase = (rows_k * cols_n % frame).astype(jnp.float32) * (2.0 * jnp.pi / frame)
    return jnp.concatenate([jnp.cos(phase), -jnp.sin(phase)], axis=0).astype(jnp.bfloat16)


def body(voltages, panel_map, block_list):
    frame = 2 * CHANNELS
    spec_dev = voltages.shape[0] // frame
    groups = lax.axis_size("tm")
    band_dev = CHANNELS // groups
    panel_rows = panel_map.reshape(-1, PANEL)
    columns = panel_rows[block_list]
    width = voltages.shape[1]
    frames = voltages.reshape(spec_dev, frame, width)
    earlier = from_behind(frames[spec_dev - (TAPS - 1) :], "tm", 1)
    padded = jnp.concatenate([earlier, frames], axis=0)
    coeff = filter_taps(TAPS, frame)
    filtered = jnp.zeros((spec_dev, frame, width), jnp.float32)
    for tap in range(TAPS):
        filtered = filtered + coeff[tap][None, :, None] * padded[tap : tap + spec_dev].astype(
            jnp.float32
        )
    filtered = filtered.astype(jnp.bfloat16)
    table = dft_table(CHANNELS)
    spectra = jnp.einsum("kn,sni->ski", table, filtered, preferred_element_type=jnp.float32)
    spectra = spectra.astype(jnp.bfloat16).reshape(spec_dev, 2, groups, band_dev, width)
    data = lax.all_to_all(spectra, "tm", split_axis=2, concat_axis=0, tiled=True)[:, :, 0]
    total = data.shape[0]
    first = data[:, :, :, columns[:, 0]]
    second = data[:, :, :, columns[:, 1]]
    flipped = jnp.stack([first[:, 1], -first[:, 0]], axis=1)
    real_part = jnp.einsum("sckbi,sckbj->bkij", first, second, preferred_element_type=jnp.float32)
    imag_part = jnp.einsum("sckbi,sckbj->bkij", flipped, second, preferred_element_type=jnp.float32)
    return jnp.stack([real_part, imag_part], axis=1) / total


def solution(mesh):
    in_specs = (P(("band", "tm"), None), P(), P())
    out_specs = P("band", None, "tm", None, None)
    return jax.shard_map(body, mesh=mesh, in_specs=in_specs, out_specs=out_specs, check_vma=False)
```

profile of v0, /device:TPU:13, one launch (start us, length us, event | category | flops | bytes accessed | tf_op | source)
XLA Modules:
  0.0 472.7 jit_solution(12410593673535821267)
XLA Ops:
  0.0 0.0 copy-start
  0.0 6.6 %slice.44 = bf16[1536,2048]{1,0:T(8,128)(2,1)} slice(bf16[2048,2048]{1,0:T(8,128)(2,1)} %param.3), slice={[512:2048], [0:2048]} | slice | bytes 12582912 | tf_op jit(solution)/shard_map/slice | solution.py:44
  6.6 3.7 collective-permute-start
  10.3 0.6 multiply_reduce_fusion
  11.6 0.1 broadcast_divide_fusion
  11.6 2.2 negate_convert_fusion
  13.8 64.7 %collective-permute-done = bf16[3,512,2048]{2,1,0:T(8,128)(2,1)} collective-permute-done((bf16[3,512,2048]{2,1,0:T(8,128)(2,1)}, bf16[3,512,2048]{2,1,0:T(8,128)(2,1)}, u32[]{:S(2)}, u32[]{:S(2)}) %collective-permute-start) | collective-permute-done | bytes 6291488 | tf_op jit(solution)/shard_map/ppermute | solution.py:14
  78.5 17.1 %fusion.6 = bf16[4,2048,512]{1,2,0:T(8,128)(2,1)} fusion(bf16[4,512,2048]{2,1,0:T(8,128)(2,1)} %bitcast.51, bf16[3,512,2048]{2,1,0:T(8,128)(2,1)} %collective-permute-done, f32[512]{0:T(512)S(1)} %get-tuple-element.10, f32[512]{0:T(512)S(1)} %get-tuple-element.11, f32[512]{0:T(512)S(1)} %get-tuple-element.12, f32[512]{0:T(512)S(1)} %get-tuple-element.9, ...), kind=kOutput, calls=%fused_computation.18 | convolution fusion | flops 4388290560 | bytes 23601152 | tf_op jit(solution)/shard_map/kn,sni->ski/dot_general | solution.py:54
  95.6 0.0 copy-start.2
  95.6 8.3 %copy.7 = bf16[4,2,16,16,2048]{4,3,1,0,2:T(8,128)(2,1)} copy(bf16[4,2,16,16,2048]{4,3,2,1,0:T(8,128)(2,1)} %bitcast.50) | data formatting | bytes 16777216 | tf_op jit(solution)/shard_map/reshape | solution.py:55
  103.9 7.2 %all-to-all-start = ((bf16[4,2,16,16,2048]{4,3,1,0,2:T(8,128)(2,1)}), bf16[4,2,16,16,2048]{4,3,1,0,2:T(8,128)(2,1)}, u32[]{:S(2)}, u32[]{:S(2)}) async-start(bf16[4,2,16,16,2048]{4,3,1,0,2:T(8,128)(2,1)} %copy.7), calls=%async_computation | async-start | bytes 16777216 | tf_op jit(solution)/shard_map/all_to_all | solution.py:56
  111.1 0.0 copy-done.2
  111.1 0.1 copy.8
  111.2 0.1 reshape.85
  111.3 0.0 copy-done
  111.3 0.6 gather_fusion
  112.0 181.5 %all-to-all-done = bf16[4,2,16,16,2048]{4,3,1,0,2:T(8,128)(2,1)} async-done(((bf16[4,2,16,16,2048]{4,3,1,0,2:T(8,128)(2,1)}), bf16[4,2,16,16,2048]{4,3,1,0,2:T(8,128)(2,1)}, u32[]{:S(2)}, u32[]{:S(2)}) %all-to-all-start) | async-done | bytes 8388640 | tf_op jit(solution)/shard_map/all_to_all | solution.py:56
  293.5 26.8 %copy.9 = bf16[64,2,16,2048]{0,2,3,1:T(8,128)(2,1)} copy(bf16[64,2,16,2048]{3,2,1,0:T(8,128)(2,1)} %bitcast.7) | data formatting | bytes 16777216 | tf_op jit(solution)/shard_map/squeeze | solution.py:56
  320.3 25.9 %gather_fusion.2 = bf16[2048,64,2,16]{1,3,2,0:T(8,128)(2,1)} fusion(bf16[64,2,16,2048]{0,2,3,1:T(8,128)(2,1)} %copy.9, s32[2048]{0:T(1024)S(1)} %fusion.26), kind=kCustom, calls=%fused_computation.2 | custom fusion | bytes 16785408 | tf_op jit(solution)/shard_map/gather | solution.py:59
  346.2 25.9 %gather_fusion.1 = bf16[2048,64,2,16]{1,3,2,0:T(8,128)(2,1)} fusion(bf16[64,2,16,2048]{0,2,3,1:T(8,128)(2,1)} %copy.9, s32[2048]{0:T(1024)S(1)} %fusion.24), kind=kCustom, calls=%fused_computation.1 | custom fusion | bytes 16785408 | tf_op jit(solution)/shard_map/gather | solution.py:58
  372.0 21.0 %copy.11 = bf16[16,128,64,2,16]{1,2,3,4,0:T(8,128)(2,1)} copy(bf16[16,128,64,2,16]{2,4,3,1,0:T(8,128)(2,1)} %bitcast.49) | data formatting | bytes 16777216 | tf_op jit(solution)/shard_map/gather | solution.py:58
  393.0 21.1 %copy.15 = bf16[64,2,16,16,128]{4,0,1,2,3:T(8,128)(2,1)} copy(bf16[64,2,16,16,128]{0,2,1,4,3:T(8,128)(2,1)} %bitcast.48) | data formatting | bytes 16777216 | tf_op jit(solution)/shard_map/gather | solution.py:59
  414.1 5.8 %fusion.35 = (bf16[64,1,16,16,128]{4,0,1,2,3:T(8,128)(2,1)}, bf16[64,1,16,16,128]{4,0,1,2,3:T(8,128)(2,1)}) fusion(bf16[64,2,16,16,128]{4,0,1,2,3:T(8,128)(2,1)} %bitcast.47), kind=kLoop, calls=%fused_computation.71 | loop fusion | flops 2097152 | bytes 16777216 | tf_op jit(solution)/shard_map/slice | solution.py:60
  419.9 14.4 %convolution_bitcast_fusion.1 = f32[16,1,16,128,128]{4,3,2,0,1:T(8,128)} fusion(bf16[64,2,16,16,128]{4,0,1,2,3:T(8,128)(2,1)} %copy.15, bf16[16,128,64,2,16]{1,2,3,4,0:T(8,128)(2,1)} %copy.11), kind=kOutput, calls=%fused_computation.10 | convolution fusion | flops 1073741824 | bytes 33554432 | tf_op jit(solution)/shard_map/sckbi,sckbj->bkij/dot_general | solution.py:61
  434.3 14.9 %convolution_bitcast_fusion = f32[16,1,16,128,128]{4,3,2,0,1:T(8,128)} fusion(bf16[64,2,16,16,128]{4,0,1,2,3:T(8,128)(2,1)} %copy.15, bf16[64,1,16,16,128]{4,0,1,2,3:T(8,128)(2,1)} %get-tuple-element.6, bf16[64,1,16,16,128]{4,0,1,2,3:T(8,128)(2,1)} %get-tuple-element.5), kind=kOutput, calls=%fused_computation.9 | convolution fusion | flops 1077936128 | bytes 33554432 | tf_op jit(solution)/shard_map/sckbi,sckbj->bkij/dot_general | solution.py:62
  449.2 12.2 %maximum_multiply_fusion = f32[16,2,16,128,128]{4,3,2,0,1:T(8,128)S(1)} fusion(f32[16,1,16,128,128]{4,3,2,0,1:T(8,128)} %convolution_bitcast_fusion, f32[16,1,16,128,128]{4,3,2,0,1:T(8,128)} %convolution_bitcast_fusion.1), kind=kLoop, calls=%fused_computation.3 | loop fusion | flops 16777216 | bytes 67108864 | tf_op jit(solution)/shard_map/div | solution.py:63
  461.4 0.0 copy-start.1
  461.4 11.3 %copy.17 = f32[16,2,16,128,128]{4,3,2,1,0:T(8,128)} copy(f32[16,2,16,128,128]{4,3,2,0,1:T(8,128)S(1)} %maximum_multiply_fusion) | data formatting | bytes 67108864 | tf_op jit(solution)/shard_map/div | solution.py:63
  472.7 0.0 copy-done.1
  (6 shorter events, 0.0 us)
Async XLA Ops:
  0.0 111.3 %copy-start = (s32[2048]{0:T(1024)S(1)}, s32[2048]{0:T(1024)}, u32[]{:S(2)}) copy-start(s32[2048]{0:T(1024)} %param.4) | copy-start | bytes 24580
  6.6 71.9 %collective-permute-start = (bf16[3,512,2048]{2,1,0:T(8,128)(2,1)}, bf16[3,512,2048]{2,1,0:T(8,128)(2,1)}, u32[]{:S(2)}, u32[]{:S(2)}) collective-permute-start(bf16[3,512,2048]{2,1,0:T(8,128)(2,1)} %bitcast), channel_id=1, source_target_pairs={{0,1},{1,2},{2,3},{3,4},{4,5},{5,6},{6,7},{7,8},{8,9},{9,10},{10,1... | collective-permute-start | bytes 18874376 | tf_op jit(solution)/shard_map/ppermute | solution.py:14
  95.6 15.5 %copy-start.2 = (s32[16,2]{0,1:T(2,128)S(1)}, s32[16,2]{0,1:T(2,128)}, u32[]{:S(2)}) copy-start(s32[16,2]{0,1:T(2,128)} %param.5) | copy-start | bytes 388
  103.9 189.6 %all-to-all-start = ((bf16[4,2,16,16,2048]{4,3,1,0,2:T(8,128)(2,1)}), bf16[4,2,16,16,2048]{4,3,1,0,2:T(8,128)(2,1)}, u32[]{:S(2)}, u32[]{:S(2)}) async-start(bf16[4,2,16,16,2048]{4,3,1,0,2:T(8,128)(2,1)} %copy.7), calls=%async_computation | async-start | bytes 16777216 | tf_op jit(solution)/shard_map/all_to_all | solution.py:56
  461.4 11.3 %copy-start.1 = (s32[2048]{0:T(1024)S(1)}, s32[2048]{0:T(1024)}, u32[]{:S(2)}) copy-start(s32[2048]{0:T(1024)} %param.4) | copy-start | bytes 24580
where the time goes:
time: 474 us; the launch traced here: 473 us
  waiting for transfers between devices  246 us (52%)
  local copies, waits for them, and re-layouts  148 us (31%)
  matrix products  46.3 us (10%)
  other arithmetic  20.9 us (4%)
  starting transfers between devices  10.9 us (2%)
    all_to_all x1, waiting for transfers between devices, body(): lax.all_to_all(spectra, 'tm', split_axis=2, concat_axis=0, tiled=True)  182 us
    ppermute x1, waiting for transfers between devices, from_behind(): return lax.ppermute(block, axis, route)  64.7 us
    gather x2, local copies, waits for them, and re-layouts, body(): second = data[:, :, :, columns[:, 1]]  46.9 us
    gather x2, local copies, waits for them, and re-layouts, body(): first = data[:, :, :, columns[:, 0]]  46.9 us
    squeeze x1, local copies, waits for them, and re-layouts, body(): lax.all_to_all(spectra, 'tm', split_axis=2, concat_axis=0, tiled=True)  26.8 us
    dot_general x1, matrix products, body(): jnp.einsum('kn,sni->ski', table, filtered, preferred_element_type=jnp.flo...  17.1 us
    dot_general x1, matrix products, body(): jnp.einsum('sckbi,sckbj->bkij', flipped, second, preferred_element_type=j...  14.9 us
    dot_general x1, matrix products, body(): jnp.einsum('sckbi,sckbj->bkij', first, second, preferred_element_type=jnp...  14.4 us
  transfers between devices with their start and end apart: 2, of which 2 were waited for; matrix products, arithmetic and copies ran while one was open for 1% of the time, Pallas kernels for 0%

commit v1 on v0

--- a/solution.py
+++ b/solution.py
@@ -6,6 +6,22 @@
 CHANNELS = 256
 TAPS = 4
 PANEL = 128
+
+
+def swapped_with_each(x, axis, split, join):
+    ways, here = (lax.axis_size(axis), lax.axis_index(axis))
+    width = x.shape[split] // ways
+    dims = list(x.shape)
+    dims[split] = width
+    height = dims[join]
+    dims[join] = height * ways
+    full = jnp.zeros(dims, x.dtype)
+    for mask in range(ways):
+        part = lax.dynamic_slice_in_dim(x, (here ^ mask) * width, width, axis=split)
+        if mask:
+            part = lax.ppermute(part, axis, [(d, d ^ mask) for d in range(ways)])
+        full = lax.dynamic_update_slice_in_dim(full, part, (here ^ mask) * height, axis=join)
+    return full
 
 
 def from_behind(block, axis, distance):
@@ -53,7 +69,7 @@
     table = dft_table(CHANNELS)
     spectra = jnp.einsum("kn,sni->ski", table, filtered, preferred_element_type=jnp.float32)
     spectra = spectra.astype(jnp.bfloat16).reshape(spec_dev, 2, groups, band_dev, width)
-    data = lax.all_to_all(spectra, "tm", split_axis=2, concat_axis=0, tiled=True)[:, :, 0]
+    data = swapped_with_each(spectra, "tm", 2, 0)[:, :, 0]
     total = data.shape[0]
     first = data[:, :, :, columns[:, 0]]
     second = data[:, :, :, columns[:, 1]]

time: 474 us -> 11200 us (23.63)
  local copies, waits for them, and re-layouts: 148 us -> 10900 us
    dynamic_update_slice x0 -> x16, local copies, waits for them, and re-layouts: none -> 10500 us  [swapped_with_each(): lax.dynamic_update_slice_in_dim(full, part, (here ^ mask) * height, axis=...]
    ppermute x0 -> x15, local copies, waits for them, and re-layouts: none -> 258 us  [swapped_with_each(): part = lax.ppermute(part, axis, [(d, d ^ mask) for d in range(ways)])]
    all_to_all x1 -> x0, waiting for transfers between devices: 182 us -> none  [body(): lax.all_to_all(spectra, 'tm', split_axis=2, concat_axis=0, tiled=True)]
    ppermute x0 -> x15, waiting for transfers between devices: none -> 121 us  [swapped_with_each(): part = lax.ppermute(part, axis, [(d, d ^ mask) for d in range(ways)])]
  transfers between devices with their start and end apart: 2 -> 16, of which waited for: 2 -> 7; matrix products, arithmetic and copies ran while one was open for 1% -> 90% of each run, Pallas kernels for 0% -> 0%
where the time goes in v1:
time: 11200 us; the launch traced here: 11100 us
  local copies, waits for them, and re-layouts  10900 us (97%)
  waiting for transfers between devices  186 us (2%)
    dynamic_update_slice x16, local copies, waits for them, and re-layouts, swapped_with_each(): lax.dynamic_update_slice_in_dim(full, part, (here ^ mask) * height, axis=...  10500 us
    ppermute x15, local copies, waits for them, and re-layouts, swapped_with_each(): part = lax.ppermute(part, axis, [(d, d ^ mask) for d in range(ways)])  258 us
  transfers between devices with their start and end apart: 16, of which 7 were waited for; matrix products, arithmetic and copies ran while one was open for 90% of the time, Pallas kernels for 0%

profile of v1, /device:TPU:13, one launch (start us, length us, event | category | flops | bytes accessed | tf_op | source)
XLA Modules:
  0.0 11140.5 jit_solution(15467728080952281660)
XLA Ops:
  14.0 64.5 collective-permute-done
  78.5 15.0 fusion.6
  102.3 8.7 collective-permute-done.2
  111.7 10.9 collective-permute-done.3
  129.1 26.2 collective-permute-done.6
  159.7 6.8 collective-permute-done.7
  169.2 46.1 collective-permute-done.9
  215.3 22.5 collective-permute-done.10
  239.8 16.7 copy.31
  262.6 684.8 %dynamic_update_slice.64 = bf16[64,2,16,2048]{0,2,3,1:T(8,128)(2,1)} dynamic-update-slice(bf16[64,2,16,2048]{0,2,3,1:T(8,128)(2,1)} %squeeze.42, bf16[4,2,16,2048]{0,2,3,1:T(8,128)(2,1)} %bitcast.59, s32[]{:T(128)S(6)} %select_n.167, s32[]{:T(128)} %constant.110.clone.1, s32[]{:T(128)} %constant.110.clone.1, s32[]{:T(128)} %constant.110.clone.1) | dynamic-update-slice | bytes 1048580 | tf_op jit(solution)/shard_map/dynamic_update_slice | solution.py:23
  947.4 16.7 copy.32
  964.1 684.8 %dynamic_update_slice.65 = bf16[64,2,16,2048]{0,2,3,1:T(8,128)(2,1)} dynamic-update-slice(bf16[64,2,16,2048]{0,2,3,1:T(8,128)(2,1)} %dynamic_update_slice.64, bf16[4,2,16,2048]{0,2,3,1:T(8,128)(2,1)} %bitcast.61, s32[]{:T(128)S(6)} %select_n.169, s32[]{:T(128)} %constant.110.clone.1, s32[]{:T(128)} %constant.110.clone.1, s32[]{:T(128)} %constant.110.clone.1) | dynamic-update-slice | bytes 1048580 | tf_op jit(solution)/shard_map/dynamic_update_slice | solution.py:23
  1649.0 16.7 copy.33
  1665.7 684.7 %dynamic_update_slice.66 = bf16[64,2,16,2048]{0,2,3,1:T(8,128)(2,1)} dynamic-update-slice(bf16[64,2,16,2048]{0,2,3,1:T(8,128)(2,1)} %dynamic_update_slice.65, bf16[4,2,16,2048]{0,2,3,1:T(8,128)(2,1)} %bitcast.62, s32[]{:T(128)S(6)} %select_n.171, s32[]{:T(128)} %constant.110.clone.1, s32[]{:T(128)} %constant.110.clone.1, s32[]{:T(128)} %constant.110.clone.1) | dynamic-update-slice | bytes 1048580 | tf_op jit(solution)/shard_map/dynamic_update_slice | solution.py:23
  2350.4 16.7 copy.34
  2367.2 684.7 %dynamic_update_slice.67 = bf16[64,2,16,2048]{0,2,3,1:T(8,128)(2,1)} dynamic-update-slice(bf16[64,2,16,2048]{0,2,3,1:T(8,128)(2,1)} %dynamic_update_slice.66, bf16[4,2,16,2048]{0,2,3,1:T(8,128)(2,1)} %bitcast.63, s32[]{:T(128)S(6)} %select_n.173, s32[]{:T(128)} %constant.110.clone.1, s32[]{:T(128)} %constant.110.clone.1, s32[]{:T(128)} %constant.110.clone.1) | dynamic-update-slice | bytes 1048580 | tf_op jit(solution)/shard_map/dynamic_update_slice | solution.py:23
  3051.9 16.7 copy.35
  3068.6 684.7 %dynamic_update_slice.68 = bf16[64,2,16,2048]{0,2,3,1:T(8,128)(2,1)} dynamic-update-slice(bf16[64,2,16,2048]{0,2,3,1:T(8,128)(2,1)} %dynamic_update_slice.67, bf16[4,2,16,2048]{0,2,3,1:T(8,128)(2,1)} %bitcast.64, s32[]{:T(128)S(6)} %select_n.175, s32[]{:T(128)} %constant.110.clone.1, s32[]{:T(128)} %constant.110.clone.1, s32[]{:T(128)} %constant.110.clone.1) | dynamic-update-slice | bytes 1048580 | tf_op jit(solution)/shard_map/dynamic_update_slice | solution.py:23
  3753.4 16.9 copy.36
  3770.3 684.7 %dynamic_update_slice.69 = bf16[64,2,16,2048]{0,2,3,1:T(8,128)(2,1)} dynamic-update-slice(bf16[64,2,16,2048]{0,2,3,1:T(8,128)(2,1)} %dynamic_update_slice.68, bf16[4,2,16,2048]{0,2,3,1:T(8,128)(2,1)} %bitcast.65, s32[]{:T(128)S(6)} %select_n.177, s32[]{:T(128)} %constant.110.clone.1, s32[]{:T(128)} %constant.110.clone.1, s32[]{:T(128)} %constant.110.clone.1) | dynamic-update-slice | bytes 1048580 | tf_op jit(solution)/shard_map/dynamic_update_slice | solution.py:23
  4455.0 16.7 copy.37
  4471.7 684.7 %dynamic_update_slice.70 = bf16[64,2,16,2048]{0,2,3,1:T(8,128)(2,1)} dynamic-update-slice(bf16[64,2,16,2048]{0,2,3,1:T(8,128)(2,1)} %dynamic_update_slice.69, bf16[4,2,16,2048]{0,2,3,1:T(8,128)(2,1)} %bitcast.66, s32[]{:T(128)S(6)} %select_n.179, s32[]{:T(128)} %constant.110.clone.1, s32[]{:T(128)} %constant.110.clone.1, s32[]{:T(128)} %constant.110.clone.1) | dynamic-update-slice | bytes 1048580 | tf_op jit(solution)/shard_map/dynamic_update_slice | solution.py:23
  5156.5 16.7 copy.38
  5173.2 195.9 %dynamic_update_slice.71 = bf16[64,2,16,2048]{0,2,3,1:T(8,128)(2,1)} dynamic-update-slice(bf16[64,2,16,2048]{0,2,3,1:T(8,128)(2,1)} %dynamic_update_slice.70, bf16[4,2,16,2048]{0,2,3,1:T(8,128)(2,1)} %bitcast.67, s32[]{:T(128)S(6)} %select_n.181, s32[]{:T(128)} %constant.110.clone.1, s32[]{:T(128)} %constant.110.clone.1, s32[]{:T(128)} %constant.110.clone.1) | dynamic-update-slice | bytes 1048580 | tf_op jit(solution)/shard_map/dynamic_update_slice | solution.py:23
  5369.2 17.5 copy.39
  5386.7 684.7 %dynamic_update_slice.72 = bf16[64,2,16,2048]{0,2,3,1:T(8,128)(2,1)} dynamic-update-slice(bf16[64,2,16,2048]{0,2,3,1:T(8,128)(2,1)} %dynamic_update_slice.71, bf16[4,2,16,2048]{0,2,3,1:T(8,128)(2,1)} %bitcast.68, s32[]{:T(128)S(6)} %select_n.183, s32[]{:T(128)} %constant.110.clone.1, s32[]{:T(128)} %constant.110.clone.1, s32[]{:T(128)} %constant.110.clone.1) | dynamic-update-slice | bytes 1048580 | tf_op jit(solution)/shard_map/dynamic_update_slice | solution.py:23
  6071.4 17.5 copy.40
  6088.9 684.7 %dynamic_update_slice.73 = bf16[64,2,16,2048]{0,2,3,1:T(8,128)(2,1)} dynamic-update-slice(bf16[64,2,16,2048]{0,2,3,1:T(8,128)(2,1)} %dynamic_update_slice.72, bf16[4,2,16,2048]{0,2,3,1:T(8,128)(2,1)} %bitcast.69, s32[]{:T(128)S(6)} %select_n.185, s32[]{:T(128)} %constant.110.clone.1, s32[]{:T(128)} %constant.110.clone.1, s32[]{:T(128)} %constant.110.clone.1) | dynamic-update-slice | bytes 1048580 | tf_op jit(solution)/shard_map/dynamic_update_slice | solution.py:23
  6773.7 17.5 copy.41
  6791.2 684.7 %dynamic_update_slice.74 = bf16[64,2,16,2048]{0,2,3,1:T(8,128)(2,1)} dynamic-update-slice(bf16[64,2,16,2048]{0,2,3,1:T(8,128)(2,1)} %dynamic_update_slice.73, bf16[4,2,16,2048]{0,2,3,1:T(8,128)(2,1)} %bitcast.70, s32[]{:T(128)S(6)} %select_n.187, s32[]{:T(128)} %constant.110.clone.1, s32[]{:T(128)} %constant.110.clone.1, s32[]{:T(128)} %constant.110.clone.1) | dynamic-update-slice | bytes 1048580 | tf_op jit(solution)/shard_map/dynamic_update_slice | solution.py:23
  7475.9 17.5 copy.42
  7493.5 684.7 %dynamic_update_slice.75 = bf16[64,2,16,2048]{0,2,3,1:T(8,128)(2,1)} dynamic-update-slice(bf16[64,2,16,2048]{0,2,3,1:T(8,128)(2,1)} %dynamic_update_slice.74, bf16[4,2,16,2048]{0,2,3,1:T(8,128)(2,1)} %bitcast.71, s32[]{:T(128)S(6)} %select_n.189, s32[]{:T(128)} %constant.110.clone.1, s32[]{:T(128)} %constant.110.clone.1, s32[]{:T(128)} %constant.110.clone.1) | dynamic-update-slice | bytes 1048580 | tf_op jit(solution)/shard_map/dynamic_update_slice | solution.py:23
  8178.2 17.5 copy.43
  8195.7 684.7 %dynamic_update_slice.76 = bf16[64,2,16,2048]{0,2,3,1:T(8,128)(2,1)} dynamic-update-slice(bf16[64,2,16,2048]{0,2,3,1:T(8,128)(2,1)} %dynamic_update_slice.75, bf16[4,2,16,2048]{0,2,3,1:T(8,128)(2,1)} %bitcast.72, s32[]{:T(128)S(6)} %select_n.191, s32[]{:T(128)} %constant.110.clone.1, s32[]{:T(128)} %constant.110.clone.1, s32[]{:T(128)} %constant.110.clone.1) | dynamic-update-slice | bytes 1048580 | tf_op jit(solution)/shard_map/dynamic_update_slice | solution.py:23
  8880.5 17.5 copy.44
  8898.0 684.7 %dynamic_update_slice.77 = bf16[64,2,16,2048]{0,2,3,1:T(8,128)(2,1)} dynamic-update-slice(bf16[64,2,16,2048]{0,2,3,1:T(8,128)(2,1)} %dynamic_update_slice.76, bf16[4,2,16,2048]{0,2,3,1:T(8,128)(2,1)} %bitcast.73, s32[]{:T(128)S(6)} %select_n.193, s32[]{:T(128)} %constant.110.clone.1, s32[]{:T(128)} %constant.110.clone.1, s32[]{:T(128)} %constant.110.clone.1) | dynamic-update-slice | bytes 1048580 | tf_op jit(solution)/shard_map/dynamic_update_slice | solution.py:23
  9582.8 17.7 copy.45
  9600.5 684.7 %dynamic_update_slice.78 = bf16[64,2,16,2048]{0,2,3,1:T(8,128)(2,1)} dynamic-update-slice(bf16[64,2,16,2048]{0,2,3,1:T(8,128)(2,1)} %dynamic_update_slice.77, bf16[4,2,16,2048]{0,2,3,1:T(8,128)(2,1)} %bitcast.74, s32[]{:T(128)S(6)} %select_n.195, s32[]{:T(128)} %constant.110.clone.1, s32[]{:T(128)} %constant.110.clone.1, s32[]{:T(128)} %constant.110.clone.1) | dynamic-update-slice | bytes 1048580 | tf_op jit(solution)/shard_map/dynamic_update_slice | solution.py:23
  10285.2 17.5 copy.46
  10302.8 684.7 %dynamic_update_slice.79 = bf16[64,2,16,2048]{0,2,3,1:T(8,128)(2,1)} dynamic-update-slice(bf16[64,2,16,2048]{0,2,3,1:T(8,128)(2,1)} %dynamic_update_slice.78, bf16[4,2,16,2048]{0,2,3,1:T(8,128)(2,1)} %bitcast.60, s32[]{:T(128)S(6)} %select_n.197, s32[]{:T(128)} %constant.110.clone.1, s32[]{:T(128)} %constant.110.clone.1, s32[]{:T(128)} %constant.110.clone.1) | dynamic-update-slice | bytes 1048580 | tf_op jit(solution)/shard_map/dynamic_update_slice | solution.py:23
  10987.5 25.9 gather_fusion.1
  11013.4 21.1 copy.49
  11034.5 25.9 gather_fusion.2
  11060.4 21.0 copy.52
  11081.5 14.4 convolution_bitcast_fusion.1
  11101.7 14.9 convolution_bitcast_fusion
  11116.7 12.2 maximum_multiply_fusion
  11128.8 11.3 copy.54
  (59 shorter events, 50.3 us)
Async XLA Ops:
  0.0 128.5 %copy-start = (s32[2048]{0:T(1024)S(1)}, s32[2048]{0:T(1024)}, u32[]{:S(2)}) copy-start(s32[2048]{0:T(1024)} %param.4) | copy-start | bytes 24580
  6.6 71.9 collective-permute-start
  93.5 34.8 copy-start.8
  96.1 4.9 collective-permute-start.1
  97.4 13.6 collective-permute-start.2
  98.6 24.1 collective-permute-start.3
  99.1 25.9 collective-permute-start.4
  99.2 25.9 collective-permute-start.5
  100.9 0.8 copy-start.4
  101.7 53.6 collective-permute-start.6
  111.0 14.2 copy-start.2
  111.0 55.5 collective-permute-start.7
  122.6 44.1 collective-permute-start.8
  124.9 90.4 collective-permute-start.9
  125.1 112.6 %collective-permute-start.10 = (bf16[4,2,1,16,2048]{4,3,2,1,0:T(8,128)(2,1)}, bf16[4,2,1,16,2048]{4,3,2,1,0:T(8,128)(2,1)}, u32[]{:S(2)}, u32[]{:S(2)}) collective-permute-start(bf16[4,2,1,16,2048]{4,3,2,1,0:T(8,128)(2,1)} %get-tuple-element.12), channel_id=1, source_target_pairs={{0,10},{1,11},{2,8},{3,9},{4,14},{5,15},{6,12},{7,13},{8,2},{9,3},... | collective-permute-start | bytes 1572872 | tf_op jit(solution)/shard_map/ppermute | solution.py:22
  155.3 7320.7 %collective-permute-start.11 = (bf16[4,2,1,16,2048]{4,3,2,1,0:T(8,128)(2,1)}, bf16[4,2,1,16,2048]{4,3,2,1,0:T(8,128)(2,1)}, u32[]{:S(2)}, u32[]{:S(2)}) collective-permute-start(bf16[4,2,1,16,2048]{4,3,2,1,0:T(8,128)(2,1)} %get-tuple-element.11), channel_id=1, source_target_pairs={{0,11},{1,10},{2,9},{3,8},{4,15},{5,14},{6,13},{7,12},{8,3},{9,2},... | collective-permute-start | bytes 1572872 | tf_op jit(solution)/shard_map/ppermute | solution.py:22
  166.5 8011.7 %collective-permute-start.12 = (bf16[4,2,1,16,2048]{4,3,2,1,0:T(8,128)(2,1)}, bf16[4,2,1,16,2048]{4,3,2,1,0:T(8,128)(2,1)}, u32[]{:S(2)}, u32[]{:S(2)}) collective-permute-start(bf16[4,2,1,16,2048]{4,3,2,1,0:T(8,128)(2,1)} %get-tuple-element.10), channel_id=1, source_target_pairs={{0,12},{1,13},{2,14},{3,15},{4,8},{5,9},{6,10},{7,11},{8,4},{9,5},... | collective-permute-start | bytes 1572872 | tf_op jit(solution)/shard_map/ppermute | solution.py:22
  166.7 8713.8 %collective-permute-start.13 = (bf16[4,2,1,16,2048]{4,3,2,1,0:T(8,128)(2,1)}, bf16[4,2,1,16,2048]{4,3,2,1,0:T(8,128)(2,1)}, u32[]{:S(2)}, u32[]{:S(2)}) collective-permute-start(bf16[4,2,1,16,2048]{4,3,2,1,0:T(8,128)(2,1)} %get-tuple-element.9), channel_id=1, source_target_pairs={{0,13},{1,12},{2,15},{3,14},{4,9},{5,8},{6,11},{7,10},{8,5},{9,4},... | collective-permute-start | bytes 1572872 | tf_op jit(solution)/shard_map/ppermute | solution.py:22
  215.3 9367.5 %collective-permute-start.14 = (bf16[4,2,1,16,2048]{4,3,2,1,0:T(8,128)(2,1)}, bf16[4,2,1,16,2048]{4,3,2,1,0:T(8,128)(2,1)}, u32[]{:S(2)}, u32[]{:S(2)}) collective-permute-start(bf16[4,2,1,16,2048]{4,3,2,1,0:T(8,128)(2,1)} %get-tuple-element.8), channel_id=1, source_target_pairs={{0,14},{1,15},{2,12},{3,13},{4,10},{5,11},{6,8},{7,9},{8,6},{9,7},... | collective-permute-start | bytes 1572872 | tf_op jit(solution)/shard_map/ppermute | solution.py:22
  237.8 10047.5 %collective-permute-start.15 = (bf16[4,2,1,16,2048]{4,3,2,1,0:T(8,128)(2,1)}, bf16[4,2,1,16,2048]{4,3,2,1,0:T(8,128)(2,1)}, u32[]{:S(2)}, u32[]{:S(2)}) collective-permute-start(bf16[4,2,1,16,2048]{4,3,2,1,0:T(8,128)(2,1)} %get-tuple-element.7), channel_id=1, source_target_pairs={{0,15},{1,14},{2,13},{3,12},{4,11},{5,10},{6,9},{7,8},{8,7},{9,6},... | collective-permute-start | bytes 1572872 | tf_op jit(solution)/shard_map/ppermute | solution.py:22
  262.6 684.8 %copy-start.5 = (bf16[4,2,1,16,2048]{4,3,2,1,0:T(8,128)(2,1)S(1)}, bf16[4,2,1,16,2048]{4,3,2,1,0:T(8,128)(2,1)}, u32[]{:S(2)}) copy-start(bf16[4,2,1,16,2048]{4,3,2,1,0:T(8,128)(2,1)} %copy-done.4) | copy-start | bytes 1572868
  964.1 684.8 %copy-start.3 = (bf16[4,2,1,16,2048]{4,3,2,1,0:T(8,128)(2,1)S(1)}, bf16[4,2,1,16,2048]{4,3,2,1,0:T(8,128)(2,1)}, u32[]{:S(2)}) copy-start(bf16[4,2,1,16,2048]{4,3,2,1,0:T(8,128)(2,1)} %copy-done.2) | copy-start | bytes 1572868
  10302.8 684.8 %copy-start.7 = (s32[2048]{0:T(1024)S(1)}, s32[2048]{0:T(1024)}, u32[]{:S(2)}) copy-start(s32[2048]{0:T(1024)} %fusion.24) | copy-start | bytes 24580
  11013.4 21.1 copy-start.6
  11128.8 11.3 copy-start.1
